TPU v7x, 32 devices: a whole 2x2x4 slice. The times are simulated.
32 devices in a mesh: az: 16 (over z, x, core), el: 2 (over y).
Axes of the slice: x: 2, y: 2, z: 4, core: 2. Of those that a mesh axis runs over, the one named last changes fastest.
Arguments:
- raw_sweeps: bfloat16 [4, 1, 24, 96, 256], P('el', None, None, 'az'), may hold values from -6 to 6
- sweep_ids: int32 [4], P('el'), may hold values from 0 to 3, each once
- elevation_embed: float32 [4, 128], replicated, may hold values from -3 to 3
- input_proj: bfloat16 [24, 128], replicated, may hold values from -0.875 to 0.875
- first_kernel: bfloat16 [3, 3, 128, 128], replicated, may hold values from -0.1875 to 0.1875
- second_kernel: bfloat16 [3, 3, 128, 128], replicated, may hold values from -0.1875 to 0.1875
- join_weight: bfloat16 [2, 128, 128], P('el'), may hold values from -0.375 to 0.375
- head_weight: bfloat16 [12, 128], replicated, may hold values from -0.5 to 0.5
- cotangent: bfloat16 [1, 12, 96, 256], P(None, None, 'az'), may hold values from -6 to 6
Outputs:
- prediction: float32 [1, 12, 96, 256], P(None, None, 'az')
- join_grad: float32 [2, 128, 128], P('el')
- first_kernel_gradient: float32 [3, 3, 128, 128], replicated
- second_kernel_gradient: float32 [3, 3, 128, 128], replicated
- input_grad: float32 [24, 128], replicated
- embed_grad: float32 [4, 128], replicated
Inputs may be any that keep to these rules, and one draw needn't show every extreme that they name: `sweep_ids`: each sweep fills exactly one slot.
All inputs are finite; a program needn't handle non-finite values.
Results may differ from a plain program's by a relative error of at most 0.023.
Values may be sent and summed in bfloat16 or wider, within the bound.
A program may use at most 64 MiB of HBM per device.

v0:
```python
import math
import jax
import jax.numpy as jnp
from jax import lax
from jax.sharding import PartitionSpec as P

CHANNELS = 128
FIRST_DILATION = 1
SECOND_DILATION = 2
precise = lax.Precision.HIGHEST


def padded_2(block, sides, width):
    for axis, dim in sides:
        count = lax.axis_size(axis)
        forward = [(i, i + 1) for i in range(count - 1)]
        forward.append((count - 1, 0))
        backward = [(target, source) for source, target in forward]
        low = lax.ppermute(
            lax.slice_in_dim(block, block.shape[dim] - width, None, axis=dim), axis, forward
        )
        high = lax.ppermute(lax.slice_in_dim(block, 0, width, axis=dim), axis, backward)
        block = jnp.concatenate([low, block, high], axis=dim)
    return block


def silu_slope(values):
    logistic = jax.nn.sigmoid(values)
    return logistic * (1.0 + values * (1.0 - logistic))


def range_padding(source, dilate):
    return jnp.pad(source, ((0, 0), (0, 0), (0, 0), (dilate, dilate)))


def convolve_partial(padded, kernel, dilate):
    return lax.conv_general_dilated(
        padded,
        kernel,
        (1, 1),
        "VALID",
        rhs_dilation=(dilate, dilate),
        dimension_numbers=("NCHW", "HWIO", "NCHW"),
        preferred_element_type=jnp.float32,
    )


def reversed_kernel(kernel):
    return jnp.flip(kernel, (0, 1)).transpose(0, 1, 3, 2)


def kernel_gradient_of(padded, upstream, dilate):
    ray_count = upstream.shape[2]
    gate_count = upstream.shape[3]
    tap_rows = []
    for tap_row in range(3):
        tap_line = []
        for tap_column in range(3):
            window = padded[
                :,
                :,
                tap_row * dilate : tap_row * dilate + ray_count,
                tap_column * dilate : tap_column * dilate + gate_count,
            ]
            tap_line.append(
                jnp.einsum("niar,noar->io", window, upstream, preferred_element_type=jnp.float32)
            )
        tap_rows.append(jnp.stack(tap_line))
    return jnp.stack(tap_rows)


def activate(source):
    return jax.nn.silu(source.astype(jnp.float32)).astype(jnp.bfloat16)


def shards(
    raw_sweeps,
    sweep_ids,
    elevation_embed,
    input_proj,
    first_kernel,
    second_kernel,
    join_weight,
    head_weight,
    cotangent,
):
    brain_float_half = jnp.bfloat16
    sweep_total = elevation_embed.shape[0]
    onehot = (sweep_ids[:, None] == jnp.arange(sweep_total, dtype=jnp.int32)[None, :]).astype(
        jnp.float32
    )
    bias_rows = jnp.dot(onehot, elevation_embed, precision=precise)
    group_bias = jnp.sum(bias_rows, axis=0)
    input_state = jnp.einsum(
        "jbiar,ic->bcar", raw_sweeps, input_proj, preferred_element_type=jnp.float32
    )
    input_state = (input_state + group_bias[None, :, None, None]).astype(brain_float_half)
    input_activation = activate(input_state)
    padded_input = range_padding(
        padded_2(input_activation, (("az", 2),), FIRST_DILATION), FIRST_DILATION
    )
    hidden_state = (
        input_state.astype(jnp.float32)
        + convolve_partial(padded_input, first_kernel, FIRST_DILATION)
    ).astype(brain_float_half)
    hidden_activation = activate(hidden_state)
    padded_hidden = range_padding(
        padded_2(hidden_activation, (("az", 2),), SECOND_DILATION), SECOND_DILATION
    )
    final_state = (
        hidden_state.astype(jnp.float32)
        + convolve_partial(padded_hidden, second_kernel, SECOND_DILATION)
    ).astype(brain_float_half)
    group_weight = join_weight[0]
    empty_sum = jnp.zeros((CHANNELS,) + final_state.shape[:1] + final_state.shape[2:], jnp.float32)
    joined_all = (
        empty_sum
        + jnp.einsum(
            "gbiar,gio->obar",
            lax.all_gather(final_state[None], "el", axis=0, tiled=True),
            lax.all_gather(join_weight, "el", axis=0, tiled=True),
            preferred_element_type=jnp.float32,
        )
    ).astype(brain_float_half)
    prediction = jnp.einsum(
        "lc,cbar->blar", head_weight, joined_all, preferred_element_type=jnp.float32
    )
    ray_total = final_state.shape[2] * lax.axis_size("az")
    grad_scale = 1.0 / math.sqrt(
        lax.axis_size("el") * final_state.shape[0] * ray_total * final_state.shape[3]
    )
    joined_back = jnp.einsum(
        "lc,blar->bcar", head_weight, cotangent, preferred_element_type=jnp.float32
    ).astype(brain_float_half)
    join_local = jnp.einsum(
        "biar,boar->io", final_state, joined_back, preferred_element_type=jnp.float32
    )
    join_total = lax.psum(join_local, "az")
    grad_two = jnp.einsum(
        "io,boar->biar", group_weight, joined_back, preferred_element_type=jnp.float32
    )
    final_upstream_gradient = grad_two.astype(brain_float_half)
    second_kernel_partial = kernel_gradient_of(
        padded_hidden, final_upstream_gradient, SECOND_DILATION
    )
    second_border_rays = range_padding(
        padded_2(final_upstream_gradient, (("az", 2),), SECOND_DILATION), SECOND_DILATION
    )
    second_backward_pass = convolve_partial(
        second_border_rays, reversed_kernel(second_kernel), SECOND_DILATION
    )
    grad_one = grad_two + second_backward_pass * silu_slope(hidden_state.astype(jnp.float32))
    hidden_upstream_gradient = grad_one.astype(brain_float_half)
    first_kernel_partial = kernel_gradient_of(
        padded_input, hidden_upstream_gradient, FIRST_DILATION
    )
    first_border_rays = range_padding(
        padded_2(hidden_upstream_gradient, (("az", 2),), FIRST_DILATION), FIRST_DILATION
    )
    first_backward_pass = convolve_partial(
        first_border_rays, reversed_kernel(first_kernel), FIRST_DILATION
    )
    grad_zero = (
        grad_one + first_backward_pass * silu_slope(input_state.astype(jnp.float32))
    ).astype(brain_float_half)
    input_local = jnp.einsum(
        "jbiar,bcar->ic", raw_sweeps, grad_zero, preferred_element_type=jnp.float32
    )
    column_sum = jnp.sum(grad_zero.astype(jnp.float32), axis=(0, 2, 3))
    slot_terms = jnp.broadcast_to(column_sum[None, :], (raw_sweeps.shape[0], column_sum.shape[0]))
    embed_local = jnp.dot(onehot.T, slot_terms, precision=precise)
    second_total, first_total, input_total, embed_total = lax.psum(
        (second_kernel_partial, first_kernel_partial, input_local, embed_local), ("az", "el")
    )
    return (
        prediction,
        join_total[None] * grad_scale,
        first_total * grad_scale,
        second_total * grad_scale,
        input_total * grad_scale,
        embed_total * grad_scale,
    )


def solution(mesh):
    in_specs = (
        P("el", None, None, "az", None),
        P("el"),
        P(),
        P(),
        P(),
        P(),
        P("el", None, None),
        P(),
        P(None, None, "az", None),
    )
    out_specs = (P(None, None, "az", None), P("el", None, None), P(), P(), P(), P())
    return jax.shard_map(shards, mesh=mesh, in_specs=in_specs, out_specs=out_specs, check_vma=False)
```

profile of v0, /device:TPU:0, one launch (start us, length us, event | category | flops | bytes accessed | tf_op | source)
XLA Modules:
  0.0 342.1 jit_solution(14312674388534561637)
XLA Ops:
  7.2 1.0 convert_reduce_fusion.1
  9.1 1.9 fusion.30
  11.6 5.0 %collective-permute-start.1 = (bf16[1,128,1,256]{1,3,2,0:T(8,128)(2,1)S(1)}, bf16[1,128,1,256]{1,3,2,0:T(8,128)(2,1)S(1)}, u32[]{:S(2)}, u32[]{:S(2)}) collective-permute-start(bf16[1,128,1,256]{1,3,2,0:T(8,128)(2,1)S(1)} %get-tuple-element.42), channel_id=1, source_target_pairs={{2,0},{4,2},{6,4},{8,6},{10,8},{12,10},{14,12},{16,14},{18,16},{20... | collective-permute-start | bytes 196616 | tf_op jit(solution)/shard_map/ppermute | solution.py:22
  16.9 1.2 fusion.177
  18.2 4.4 %collective-permute-start.5 = (bf16[1,128,2,256]{1,3,2,0:T(8,128)(2,1)S(1)}, bf16[1,128,2,256]{1,3,2,0:T(8,128)(2,1)S(1)}, u32[]{:S(2)}, u32[]{:S(2)}) collective-permute-start(bf16[1,128,2,256]{1,3,2,0:T(8,128)(2,1)S(1)} %get-tuple-element.44), channel_id=1, source_target_pairs={{2,0},{4,2},{6,4},{8,6},{10,8},{12,10},{14,12},{16,14},{18,16},{20... | collective-permute-start | bytes 393224 | tf_op jit(solution)/shard_map/ppermute | solution.py:22
  22.6 4.7 %all_gather.7 = bf16[2,128,128]{2,1,0:T(8,128)(2,1)} all-gather(bf16[1,128,128]{2,1,0:T(8,128)(2,1)S(1)} %copy-done.10), channel_id=1, replica_groups=mesh['az'=16,'el'=2] {'el'}, dimensions={0}, use_global_device_ids=true | all-gather | bytes 98304 | tf_op jit(solution)/shard_map/all_gather | solution.py:121
  28.6 1.1 convolution_select_fusion.3
  29.9 1.0 reshape.182
  32.4 1.1 convolution_select_fusion.1
  34.6 3.1 fusion.170
  41.6 4.4 %collective-permute-start.7 = (bf16[1,128,1,256]{1,3,2,0:T(8,128)(2,1)S(1)}, bf16[1,128,1,256]{1,3,2,0:T(8,128)(2,1)S(1)}, u32[]{:S(2)}, u32[]{:S(2)}) collective-permute-start(bf16[1,128,1,256]{1,3,2,0:T(8,128)(2,1)S(1)} %get-tuple-element.38), channel_id=1, source_target_pairs={{2,0},{4,2},{6,4},{8,6},{10,8},{12,10},{14,12},{16,14},{18,16},{20... | collective-permute-start | bytes 196616 | tf_op jit(solution)/shard_map/ppermute | solution.py:22
  46.0 4.4 %collective-permute-start.3 = (bf16[1,128,2,256]{1,3,2,0:T(8,128)(2,1)S(1)}, bf16[1,128,2,256]{1,3,2,0:T(8,128)(2,1)S(1)}, u32[]{:S(2)}, u32[]{:S(2)}) collective-permute-start(bf16[1,128,2,256]{1,3,2,0:T(8,128)(2,1)S(1)} %get-tuple-element.40), channel_id=1, source_target_pairs={{2,0},{4,2},{6,4},{8,6},{10,8},{12,10},{14,12},{16,14},{18,16},{20... | collective-permute-start | bytes 393224 | tf_op jit(solution)/shard_map/ppermute | solution.py:22
  52.6 1.1 convolution_select_fusion
  53.9 1.0 reshape.188
  54.8 2.0 convert_reduce_fusion
  57.2 37.2 %all-reduce.2 = (f32[24,128]{1,0:T(8,128)S(1)}, f32[4,128]{1,0:T(4,128)S(1)}) all-reduce(f32[24,128]{1,0:T(8,128)S(1)} %convolution_bitcast_fusion.21, f32[4,128]{1,0:T(4,128)S(1)} %fusion.135), channel_id=1, replica_groups=mesh['az'=16,'el'=2] {'az','el'}, use_global_device_ids=true, to_apply=%region_5.6 | all-reduce | flops 3584 | bytes 28672 | tf_op jit(solution)/shard_map/psum | solution.py:172
  101.5 1.1 convolution_select_fusion.2
  102.8 1.0 reshape.184
  103.8 1.2 fusion.15
  108.6 11.7 %all-gather = bf16[2,128,6,256]{3,1,2,0:T(8,128)(2,1)S(1)} all-gather(bf16[1,128,6,256]{3,1,2,0:T(8,128)(2,1)S(1)} %copy.130), channel_id=2, replica_groups=mesh['az'=16,'el'=2] {'el'}, dimensions={0}, use_global_device_ids=true | all-gather | bytes 1179648 | tf_op jit(solution)/shard_map/all_gather | solution.py:120
  121.8 70.7 %all-reduce.7.cloned.1.call-done = f32[128,128]{1,0:T(8,128)} async-done(((f32[128,128]{1,0:T(8,128)}), f32[128,128]{1,0:T(8,128)}) %all-reduce.7.cloned.1.call-update) | async-done | bytes 65552 | tf_op jit(solution)/shard_map/psum | solution.py:138
  192.5 1.5 multiply_bitcast_fusion
  193.9 138.5 %all-reduce.9.cloned.1.call-done = (f32[3,3,128,128]{3,2,1,0:T(8,128)}, f32[3,3,128,128]{3,2,1,0:T(8,128)}) async-done(((f32[3,3,128,128]{3,2,1,0:T(8,128)}, f32[3,3,128,128]{3,2,1,0:T(8,128)}), (f32[3,3,128,128]{3,2,1,0:T(8,128)}, f32[3,3,128,128]{3,2,1,0:T(8,128)})) %all-reduce.9.cloned.1.call-update) | async-done | bytes 1179664 | tf_op jit(solution)/shard_map/psum | solution.py:172
  332.4 2.0 broadcast_multiply_fusion
  (127 shorter events, 25.1 us)
Async XLA Ops:
  7.2 20.9 %copy-start = (bf16[3,3,128,128]{3,2,1,0:T(8,128)(2,1)S(1)}, bf16[3,3,128,128]{3,2,1,0:T(8,128)(2,1)}, u32[]{:S(2)}) copy-start(bf16[3,3,128,128]{3,2,1,0:T(8,128)(2,1)} %param.13) | copy-start | bytes 884740
  7.2 185.3 %all-reduce.7.cloned.1.call-start = ((), (), s32[]{:S(2)}) async-start(), calls=%async_computation | async-start | bytes 131072 | tf_op jit(solution)/shard_map/psum | solution.py:138
  9.1 7.5 %copy-start.17 = (bf16[1,12,6,256]{3,2,1,0:T(8,128)(2,1)S(1)}, bf16[1,12,6,256]{3,2,1,0:T(8,128)(2,1)}, u32[]{:S(2)}) copy-start(bf16[1,12,6,256]{3,2,1,0:T(8,128)(2,1)} %param.17) | copy-start | bytes 110596
  9.1 7.5 %copy-start.18 = (bf16[12,128]{1,0:T(8,128)(2,1)S(1)}, bf16[12,128]{1,0:T(8,128)(2,1)}, u32[]{:S(2)}) copy-start(bf16[12,128]{1,0:T(8,128)(2,1)} %param.16) | copy-start | bytes 9220
  9.1 7.8 %copy-start.10 = (bf16[1,128,128]{2,1,0:T(8,128)(2,1)S(1)}, bf16[1,128,128]{2,1,0:T(8,128)(2,1)}, u32[]{:S(2)}) copy-start(bf16[1,128,128]{2,1,0:T(8,128)(2,1)} %param.15) | copy-start | bytes 98308
  11.1 16.2 %copy-start.1 = (bf16[128,6,256]{0,2,1:T(8,128)(2,1)}, bf16[128,6,256]{0,2,1:T(8,128)(2,1)S(1)}, u32[]{:S(2)}) copy-start(bf16[128,6,256]{0,2,1:T(8,128)(2,1)S(1)} %get-tuple-element.47) | copy-start | bytes 1179652
  11.1 16.2 %collective-permute-start = (bf16[1,128,1,256]{1,3,2,0:T(8,128)(2,1)S(1)}, bf16[1,128,1,256]{1,3,2,0:T(8,128)(2,1)S(1)}, u32[]{:S(2)}, u32[]{:S(2)}) collective-permute-start(bf16[1,128,1,256]{1,3,2,0:T(8,128)(2,1)S(1)} %get-tuple-element.41), channel_id=1, source_target_pairs={{0,2},{2,4},{4,6},{6,8},{8,10},{10,12},{12,14},{14,16},{16,18},{18... | collective-permute-start | bytes 196616 | tf_op jit(solution)/shard_map/ppermute | solution.py:19
  11.6 15.7 %collective-permute-start.1 = (bf16[1,128,1,256]{1,3,2,0:T(8,128)(2,1)S(1)}, bf16[1,128,1,256]{1,3,2,0:T(8,128)(2,1)S(1)}, u32[]{:S(2)}, u32[]{:S(2)}) collective-permute-start(bf16[1,128,1,256]{1,3,2,0:T(8,128)(2,1)S(1)} %get-tuple-element.42), channel_id=1, source_target_pairs={{2,0},{4,2},{6,4},{8,6},{10,8},{12,10},{14,12},{16,14},{18,16},{20... | collective-permute-start | bytes 196616 | tf_op jit(solution)/shard_map/ppermute | solution.py:22
  18.1 12.8 %collective-permute-start.4 = (bf16[1,128,2,256]{1,3,2,0:T(8,128)(2,1)S(1)}, bf16[1,128,2,256]{1,3,2,0:T(8,128)(2,1)S(1)}, u32[]{:S(2)}, u32[]{:S(2)}) collective-permute-start(bf16[1,128,2,256]{1,3,2,0:T(8,128)(2,1)S(1)} %get-tuple-element.43), channel_id=1, source_target_pairs={{0,2},{2,4},{4,6},{6,8},{8,10},{10,12},{12,14},{14,16},{16,18},{18... | collective-permute-start | bytes 393224 | tf_op jit(solution)/shard_map/ppermute | solution.py:19
  18.2 12.7 %collective-permute-start.5 = (bf16[1,128,2,256]{1,3,2,0:T(8,128)(2,1)S(1)}, bf16[1,128,2,256]{1,3,2,0:T(8,128)(2,1)S(1)}, u32[]{:S(2)}, u32[]{:S(2)}) collective-permute-start(bf16[1,128,2,256]{1,3,2,0:T(8,128)(2,1)S(1)} %get-tuple-element.44), channel_id=1, source_target_pairs={{2,0},{4,2},{6,4},{8,6},{10,8},{12,10},{14,12},{16,14},{18,16},{20... | collective-permute-start | bytes 393224 | tf_op jit(solution)/shard_map/ppermute | solution.py:22
  39.5 1.0 copy-start.2
  40.9 9.6 %copy-start.16 = (bf16[1,128,1,256]{1,3,2,0:T(8,128)(2,1)S(1)}, bf16[1,128,1,256]{1,3,2,0:T(8,128)(2,1)}, u32[]{:S(2)}) copy-start(bf16[1,128,1,256]{1,3,2,0:T(8,128)(2,1)} %copy-done.15) | copy-start | bytes 196612
  41.5 10.5 %collective-permute-start.6 = (bf16[1,128,1,256]{1,3,2,0:T(8,128)(2,1)S(1)}, bf16[1,128,1,256]{1,3,2,0:T(8,128)(2,1)S(1)}, u32[]{:S(2)}, u32[]{:S(2)}) collective-permute-start(bf16[1,128,1,256]{1,3,2,0:T(8,128)(2,1)S(1)} %get-tuple-element.37), channel_id=1, source_target_pairs={{0,2},{2,4},{4,6},{6,8},{8,10},{10,12},{12,14},{14,16},{16,18},{18... | collective-permute-start | bytes 196616 | tf_op jit(solution)/shard_map/ppermute | solution.py:19
  41.6 10.4 %collective-permute-start.7 = (bf16[1,128,1,256]{1,3,2,0:T(8,128)(2,1)S(1)}, bf16[1,128,1,256]{1,3,2,0:T(8,128)(2,1)S(1)}, u32[]{:S(2)}, u32[]{:S(2)}) collective-permute-start(bf16[1,128,1,256]{1,3,2,0:T(8,128)(2,1)S(1)} %get-tuple-element.38), channel_id=1, source_target_pairs={{2,0},{4,2},{6,4},{8,6},{10,8},{12,10},{14,12},{16,14},{18,16},{20... | collective-permute-start | bytes 196616 | tf_op jit(solution)/shard_map/ppermute | solution.py:22
  46.0 49.1 %collective-permute-start.2 = (bf16[1,128,2,256]{1,3,2,0:T(8,128)(2,1)S(1)}, bf16[1,128,2,256]{1,3,2,0:T(8,128)(2,1)S(1)}, u32[]{:S(2)}, u32[]{:S(2)}) collective-permute-start(bf16[1,128,2,256]{1,3,2,0:T(8,128)(2,1)S(1)} %get-tuple-element.39), channel_id=1, source_target_pairs={{0,2},{2,4},{4,6},{6,8},{8,10},{10,12},{12,14},{14,16},{16,18},{18... | collective-permute-start | bytes 393224 | tf_op jit(solution)/shard_map/ppermute | solution.py:19
  46.0 49.1 %collective-permute-start.3 = (bf16[1,128,2,256]{1,3,2,0:T(8,128)(2,1)S(1)}, bf16[1,128,2,256]{1,3,2,0:T(8,128)(2,1)S(1)}, u32[]{:S(2)}, u32[]{:S(2)}) collective-permute-start(bf16[1,128,2,256]{1,3,2,0:T(8,128)(2,1)S(1)} %get-tuple-element.40), channel_id=1, source_target_pairs={{2,0},{4,2},{6,4},{8,6},{10,8},{12,10},{14,12},{16,14},{18,16},{20... | collective-permute-start | bytes 393224 | tf_op jit(solution)/shard_map/ppermute | solution.py:22
  54.8 2.2 copy-start.21
  103.8 2.3 copy-start.14
  105.1 1.4 copy-start.6
  105.1 1.4 copy-start.7
  105.1 1.4 copy-start.12
  106.1 226.3 %all-reduce.9.cloned.1.call-start = ((), (), s32[]{:S(2)}) async-start(), calls=%async_computation.1 | async-start | bytes 2359296 | tf_op jit(solution)/shard_map/psum | solution.py:172
  108.5 11.9 %copy-start.9 = (bf16[2,128,128]{2,1,0:T(8,128)(2,1)S(1)}, bf16[2,128,128]{2,1,0:T(8,128)(2,1)}, u32[]{:S(2)}) copy-start(bf16[2,128,128]{2,1,0:T(8,128)(2,1)} %all_gather.7) | copy-start | bytes 196612
  332.4 2.0 copy-start.3
  (9 other events, 7.2 us)
Sparse Core Ops, SparseCore 0:
  106.2 86.2 all-reduce.6
  199.5 132.8 all-reduce.8
where the time goes:
time: 343 us; the launch traced here: 342 us
  waiting for transfers between devices  209 us (61%)
  blocking collectives  53.6 us (16%)
  matrix products  19.5 us (6%)
  starting transfers between devices  19 us (6%)
  other arithmetic  15.1 us (4%)
  between operations  14.6 us (4%)
  local copies, waits for them, and re-layouts  11 us (3%)
    psum x1, waiting for transfers between devices, shards(): lax.psum((second_kernel_partial, first_kernel_partial, input_local, embed...  138 us
    psum x1, waiting for transfers between devices, shards(): join_total = lax.psum(join_local, 'az')  70.7 us
    psum x1, blocking collectives, shards(): lax.psum((second_kernel_partial, first_kernel_partial, input_local, embed...  37.2 us
    ppermute x4, starting transfers between devices, padded_2(): lax.ppermute(lax.slice_in_dim(block, 0, width, axis=dim), axis, backward)  18.3 us
    all_gather x1, blocking collectives, shards(): lax.all_gather(final_state[None], 'el', axis=0, tiled=True)  11.7 us
    dot_general x18, matrix products, kernel_gradient_of(): jnp.einsum('niar,noar->io', window, upstream, preferred_element_type=jnp....  8.68 us
  transfers between devices with their start and end apart: 10, of which 2 were waited for; matrix products, arithmetic and copies ran while one was open for 5% of the time, Pallas kernels for 0%

commit v1 on v0

--- a/solution.py
+++ b/solution.py
@@ -169,8 +169,12 @@
     column_sum = jnp.sum(grad_zero.astype(jnp.float32), axis=(0, 2, 3))
     slot_terms = jnp.broadcast_to(column_sum[None, :], (raw_sweeps.shape[0], column_sum.shape[0]))
     embed_local = jnp.dot(onehot.T, slot_terms, precision=precise)
-    second_total, first_total, input_total, embed_total = lax.psum(
-        (second_kernel_partial, first_kernel_partial, input_local, embed_local), ("az", "el")
+
+    def _choose_masks(field_in):
+        return lax.psum(lax.psum(field_in, "el"), "az")
+
+    second_total, first_total, input_total, embed_total = _choose_masks(
+        (second_kernel_partial, first_kernel_partial, input_local, embed_local)
     )
     return (
         prediction,

time: 343 us -> 237 us (0.69)
  waiting for transfers between devices: 209 us -> 79.5 us
  blocking collectives: 53.6 us -> 80 us
    psum x1, waiting for transfers between devices: 138 us -> 0.01 us  [_choose_masks(): return lax.psum(lax.psum(field_in, 'el'), 'az')]
    psum x1 -> x2, blocking collectives: 37.2 us -> 66.9 us  [_choose_masks(): return lax.psum(lax.psum(field_in, 'el'), 'az')]
    psum x1, waiting for transfers between devices: 70.7 us -> 79.4 us  [shards(): join_total = lax.psum(join_local, 'az')]
  transfers between devices with their start and end apart: 10 -> 10, of which waited for: 2 -> 1; matrix products, arithmetic and copies ran while one was open for 5% -> 7% of each run, Pallas kernels for 0% -> 0%
where the time goes in v1:
time: 237 us
  blocking collectives  80 us (34%)
  waiting for transfers between devices  79.5 us (34%)
  starting transfers between devices  19 us (8%)
  matrix products  17.1 us (7%)
  between operations  14.5 us (6%)
  local copies, waits for them, and re-layouts  14.2 us (6%)
  other arithmetic  12.4 us (5%)
    psum x1, waiting for transfers between devices, shards(): join_total = lax.psum(join_local, 'az')  79.4 us
    psum x2, blocking collectives, _choose_masks(): return lax.psum(lax.psum(field_in, 'el'), 'az')  66.9 us
    ppermute x4, starting transfers between devices, padded_2(): lax.ppermute(lax.slice_in_dim(block, 0, width, axis=dim), axis, backward)  18.3 us
    all_gather x1, blocking collectives, shards(): lax.all_gather(final_state[None], 'el', axis=0, tiled=True)  8.45 us
    dot_general x18, matrix products, kernel_gradient_of(): jnp.einsum('niar,noar->io', window, upstream, preferred_element_type=jnp....  6.18 us
    conv_general_dilated x18, local copies, waits for them, and re-layouts, convolve_partial(): lax.conv_general_dilated(padded, kernel, (1, 1), 'VALID', rhs_dilation=(d...  5.56 us
    unnamed x41, local copies, waits for them, and re-layouts  5.37 us
  transfers between devices with their start and end apart: 10, of which 1 were waited for; matrix products, arithmetic and copies ran while one was open for 7% of the time, Pallas kernels for 0%

profile of v1, /device:TPU:0, one launch (start us, length us, event | category | flops | bytes accessed | tf_op | source)
XLA Modules:
  0.0 236.6 jit_solution(4627080914017092833)
XLA Ops:
  7.2 1.0 convert_reduce_fusion.1
  9.1 1.9 fusion.30
  11.6 5.0 %collective-permute-start.1 = (bf16[1,128,1,256]{1,3,2,0:T(8,128)(2,1)S(1)}, bf16[1,128,1,256]{1,3,2,0:T(8,128)(2,1)S(1)}, u32[]{:S(2)}, u32[]{:S(2)}) collective-permute-start(bf16[1,128,1,256]{1,3,2,0:T(8,128)(2,1)S(1)} %get-tuple-element.47), channel_id=1, source_target_pairs={{2,0},{4,2},{6,4},{8,6},{10,8},{12,10},{14,12},{16,14},{18,16},{20... | collective-permute-start | bytes 196616 | tf_op jit(solution)/shard_map/ppermute | solution.py:22
  16.9 1.2 fusion.177
  18.9 4.4 %collective-permute-start.5 = (bf16[1,128,2,256]{1,3,2,0:T(8,128)(2,1)}, bf16[1,128,2,256]{1,3,2,0:T(8,128)(2,1)S(1)}, u32[]{:S(2)}, u32[]{:S(2)}) collective-permute-start(bf16[1,128,2,256]{1,3,2,0:T(8,128)(2,1)} %get-tuple-element.49), channel_id=1, source_target_pairs={{2,0},{4,2},{6,4},{8,6},{10,8},{12,10},{14,12},{16,14},{18,16},{20... | collective-permute-start | bytes 393224 | tf_op jit(solution)/shard_map/ppermute | solution.py:22
  23.3 4.7 %all_gather.7 = bf16[2,128,128]{2,1,0:T(8,128)(2,1)} all-gather(bf16[1,128,128]{2,1,0:T(8,128)(2,1)S(1)} %copy-done.9), channel_id=1, replica_groups=mesh['az'=16,'el'=2] {'el'}, dimensions={0}, use_global_device_ids=true | all-gather | bytes 98304 | tf_op jit(solution)/shard_map/all_gather | solution.py:121
  29.3 1.1 convolution_select_fusion.3
  30.6 1.0 reshape.182
  31.7 1.0 pad.16
  32.7 1.3 reshape.173
  35.0 1.1 convolution_select_fusion.1
  36.3 1.0 reshape.186
  37.3 3.1 %fusion.170 = (bf16[1,128,6,256]{1,3,2,0:T(8,128)(2,1)S(1)}, f32[1,128,6,256]{1,3,2,0:T(8,128)}, bf16[1,128,6,256]{1,3,2,0:T(8,128)(2,1)S(1)}) fusion(f32[1,128,6,256]{1,3,2,0:T(8,128)} %get-tuple-element.51, f32[6,1,264,128]{3,2,0,1:T(8,128)} %reshape.186, f32[6,1,264,128]{3,2,0,1:T(8,128)} %reshape.182, f32[6,256,128]{2,1,0:T(8,128)} %get-tuple-element.53), kind=kLoop, calls=%fused_computation.226 | loop fusion | flops 2555904 | bytes 4718592 | tf_op jit(solution)/shard_map/convert_element_type | solution.py:153
  44.2 4.4 %collective-permute-start.7 = (bf16[1,128,1,256]{1,3,2,0:T(8,128)(2,1)S(1)}, bf16[1,128,1,256]{1,3,2,0:T(8,128)(2,1)S(1)}, u32[]{:S(2)}, u32[]{:S(2)}) collective-permute-start(bf16[1,128,1,256]{1,3,2,0:T(8,128)(2,1)S(1)} %get-tuple-element.43), channel_id=1, source_target_pairs={{2,0},{4,2},{6,4},{8,6},{10,8},{12,10},{14,12},{16,14},{18,16},{20... | collective-permute-start | bytes 196616 | tf_op jit(solution)/shard_map/ppermute | solution.py:22
  48.6 4.4 %collective-permute-start.3 = (bf16[1,128,2,256]{1,3,2,0:T(8,128)(2,1)S(1)}, bf16[1,128,2,256]{1,3,2,0:T(8,128)(2,1)S(1)}, u32[]{:S(2)}, u32[]{:S(2)}) collective-permute-start(bf16[1,128,2,256]{1,3,2,0:T(8,128)(2,1)S(1)} %get-tuple-element.45), channel_id=1, source_target_pairs={{2,0},{4,2},{6,4},{8,6},{10,8},{12,10},{14,12},{16,14},{18,16},{20... | collective-permute-start | bytes 393224 | tf_op jit(solution)/shard_map/ppermute | solution.py:22
  55.2 1.1 convolution_select_fusion
  56.5 1.0 reshape.188
  63.9 8.7 %all-reduce.4 = (f32[24,128]{1,0:T(8,128)S(1)}, f32[4,128]{1,0:T(4,128)S(1)}) all-reduce(f32[24,128]{1,0:T(8,128)S(1)} %convolution_bitcast_fusion.21, f32[4,128]{1,0:T(4,128)S(1)} %fusion.135), channel_id=1, replica_groups=mesh['az'=16,'el'=2] {'el'}, use_global_device_ids=true, to_apply=%region_7.8 | all-reduce | flops 3584 | bytes 28672 | tf_op jit(solution)/shard_map/psum | solution.py:174
  72.5 58.2 %all-reduce.2 = (f32[24,128]{1,0:T(8,128)S(1)}, f32[4,128]{1,0:T(4,128)S(1)}) all-reduce(f32[24,128]{1,0:T(8,128)S(1)} %get-tuple-element.29, f32[4,128]{1,0:T(4,128)S(1)} %get-tuple-element.30), channel_id=1, replica_groups=mesh['az'=16,'el'=2] {'az'}, use_global_device_ids=true, to_apply=%region_8.9 | all-reduce | flops 3584 | bytes 28672 | tf_op jit(solution)/shard_map/psum | solution.py:174
  130.7 1.3 pad.14
  133.2 1.1 convolution_select_fusion.2
  137.0 8.5 %all-gather = bf16[2,128,6,256]{3,1,2,0:T(8,128)(2,1)S(1)} all-gather(bf16[1,128,6,256]{3,1,2,0:T(8,128)(2,1)S(1)} %copy.130), channel_id=2, replica_groups=mesh['az'=16,'el'=2] {'el'}, dimensions={0}, use_global_device_ids=true | all-gather | bytes 1179648 | tf_op jit(solution)/shard_map/all_gather | solution.py:120
  146.9 79.4 %all-reduce.9.cloned.1.call-done = (f32[128,128]{1,0:T(8,128)}, f32[3,3,128,128]{3,2,1,0:T(8,128)}, f32[3,3,128,128]{3,2,1,0:T(8,128)}) async-done(((f32[128,128]{1,0:T(8,128)}, f32[3,3,128,128]{3,2,1,0:T(8,128)}, f32[3,3,128,128]{3,2,1,0:T(8,128)}), (f32[128,128]{1,0:T(8,128)}, f32[3,3,128,128]{3,2,1,0:T(8,128)}, f32[3,3,128,128]{3,2,1,0:T(8,128)})) %all-reduce.9.cloned.1.call-update) | async-done | bytes 1245200 | tf_op jit(solution)/shard_map/psum | solution.py:138
  226.3 2.0 broadcast_multiply_fusion
  (120 shorter events, 24.2 us)
Async XLA Ops:
  7.2 21.6 %copy-start = (bf16[3,3,128,128]{3,2,1,0:T(8,128)(2,1)S(1)}, bf16[3,3,128,128]{3,2,1,0:T(8,128)(2,1)}, u32[]{:S(2)}) copy-start(bf16[3,3,128,128]{3,2,1,0:T(8,128)(2,1)} %param.13) | copy-start | bytes 884740
  7.2 128.4 %all-reduce.11.cloned.1.call-start = ((), (), s32[]{:S(2)}) async-start(), calls=%async_computation.1 | async-start | bytes 2359296 | tf_op jit(solution)/shard_map/psum | solution.py:174
  9.1 7.5 %copy-start.13 = (bf16[1,12,6,256]{3,2,1,0:T(8,128)(2,1)S(1)}, bf16[1,12,6,256]{3,2,1,0:T(8,128)(2,1)}, u32[]{:S(2)}) copy-start(bf16[1,12,6,256]{3,2,1,0:T(8,128)(2,1)} %param.17) | copy-start | bytes 110596
  9.1 7.5 %copy-start.14 = (bf16[12,128]{1,0:T(8,128)(2,1)S(1)}, bf16[12,128]{1,0:T(8,128)(2,1)}, u32[]{:S(2)}) copy-start(bf16[12,128]{1,0:T(8,128)(2,1)} %param.16) | copy-start | bytes 9220
  9.1 7.8 %copy-start.9 = (bf16[1,128,128]{2,1,0:T(8,128)(2,1)S(1)}, bf16[1,128,128]{2,1,0:T(8,128)(2,1)}, u32[]{:S(2)}) copy-start(bf16[1,128,128]{2,1,0:T(8,128)(2,1)} %param.15) | copy-start | bytes 98308
  11.1 16.9 %copy-start.4 = (bf16[128,6,256]{0,2,1:T(8,128)(2,1)}, bf16[128,6,256]{0,2,1:T(8,128)(2,1)S(1)}, u32[]{:S(2)}) copy-start(bf16[128,6,256]{0,2,1:T(8,128)(2,1)S(1)} %get-tuple-element.52) | copy-start | bytes 1179652
  11.1 16.9 %collective-permute-start = (bf16[1,128,1,256]{1,3,2,0:T(8,128)(2,1)S(1)}, bf16[1,128,1,256]{1,3,2,0:T(8,128)(2,1)S(1)}, u32[]{:S(2)}, u32[]{:S(2)}) collective-permute-start(bf16[1,128,1,256]{1,3,2,0:T(8,128)(2,1)S(1)} %get-tuple-element.46), channel_id=1, source_target_pairs={{0,2},{2,4},{4,6},{6,8},{8,10},{10,12},{12,14},{14,16},{16,18},{18... | collective-permute-start | bytes 196616 | tf_op jit(solution)/shard_map/ppermute | solution.py:19
  11.6 16.4 %collective-permute-start.1 = (bf16[1,128,1,256]{1,3,2,0:T(8,128)(2,1)S(1)}, bf16[1,128,1,256]{1,3,2,0:T(8,128)(2,1)S(1)}, u32[]{:S(2)}, u32[]{:S(2)}) collective-permute-start(bf16[1,128,1,256]{1,3,2,0:T(8,128)(2,1)S(1)} %get-tuple-element.47), channel_id=1, source_target_pairs={{2,0},{4,2},{6,4},{8,6},{10,8},{12,10},{14,12},{16,14},{18,16},{20... | collective-permute-start | bytes 196616 | tf_op jit(solution)/shard_map/ppermute | solution.py:22
  18.9 12.7 %collective-permute-start.4 = (bf16[1,128,2,256]{1,3,2,0:T(8,128)(2,1)}, bf16[1,128,2,256]{1,3,2,0:T(8,128)(2,1)S(1)}, u32[]{:S(2)}, u32[]{:S(2)}) collective-permute-start(bf16[1,128,2,256]{1,3,2,0:T(8,128)(2,1)} %get-tuple-element.48), channel_id=1, source_target_pairs={{0,2},{2,4},{4,6},{6,8},{8,10},{10,12},{12,14},{14,16},{16,18},{18... | collective-permute-start | bytes 393224 | tf_op jit(solution)/shard_map/ppermute | solution.py:19
  18.9 12.7 %collective-permute-start.5 = (bf16[1,128,2,256]{1,3,2,0:T(8,128)(2,1)}, bf16[1,128,2,256]{1,3,2,0:T(8,128)(2,1)S(1)}, u32[]{:S(2)}, u32[]{:S(2)}) collective-permute-start(bf16[1,128,2,256]{1,3,2,0:T(8,128)(2,1)} %get-tuple-element.49), channel_id=1, source_target_pairs={{2,0},{4,2},{6,4},{8,6},{10,8},{12,10},{14,12},{16,14},{18,16},{20... | collective-permute-start | bytes 393224 | tf_op jit(solution)/shard_map/ppermute | solution.py:22
  34.0 1.0 copy-start.15
  42.2 1.0 copy-start.5
  43.5 9.6 %copy-start.11 = (bf16[1,128,1,256]{1,3,2,0:T(8,128)(2,1)S(1)}, bf16[1,128,1,256]{1,3,2,0:T(8,128)(2,1)}, u32[]{:S(2)}) copy-start(bf16[1,128,1,256]{1,3,2,0:T(8,128)(2,1)} %copy-done.10) | copy-start | bytes 196612
  44.1 10.5 %collective-permute-start.6 = (bf16[1,128,1,256]{1,3,2,0:T(8,128)(2,1)S(1)}, bf16[1,128,1,256]{1,3,2,0:T(8,128)(2,1)S(1)}, u32[]{:S(2)}, u32[]{:S(2)}) collective-permute-start(bf16[1,128,1,256]{1,3,2,0:T(8,128)(2,1)S(1)} %get-tuple-element.42), channel_id=1, source_target_pairs={{0,2},{2,4},{4,6},{6,8},{8,10},{10,12},{12,14},{14,16},{16,18},{18... | collective-permute-start | bytes 196616 | tf_op jit(solution)/shard_map/ppermute | solution.py:19
  44.2 10.4 %collective-permute-start.7 = (bf16[1,128,1,256]{1,3,2,0:T(8,128)(2,1)S(1)}, bf16[1,128,1,256]{1,3,2,0:T(8,128)(2,1)S(1)}, u32[]{:S(2)}, u32[]{:S(2)}) collective-permute-start(bf16[1,128,1,256]{1,3,2,0:T(8,128)(2,1)S(1)} %get-tuple-element.43), channel_id=1, source_target_pairs={{2,0},{4,2},{6,4},{8,6},{10,8},{12,10},{14,12},{16,14},{18,16},{20... | collective-permute-start | bytes 196616 | tf_op jit(solution)/shard_map/ppermute | solution.py:22
  48.6 8.8 %collective-permute-start.2 = (bf16[1,128,2,256]{1,3,2,0:T(8,128)(2,1)S(1)}, bf16[1,128,2,256]{1,3,2,0:T(8,128)(2,1)S(1)}, u32[]{:S(2)}, u32[]{:S(2)}) collective-permute-start(bf16[1,128,2,256]{1,3,2,0:T(8,128)(2,1)S(1)} %get-tuple-element.44), channel_id=1, source_target_pairs={{0,2},{2,4},{4,6},{6,8},{8,10},{10,12},{12,14},{14,16},{16,18},{18... | collective-permute-start | bytes 393224 | tf_op jit(solution)/shard_map/ppermute | solution.py:19
  48.6 8.8 %collective-permute-start.3 = (bf16[1,128,2,256]{1,3,2,0:T(8,128)(2,1)S(1)}, bf16[1,128,2,256]{1,3,2,0:T(8,128)(2,1)S(1)}, u32[]{:S(2)}, u32[]{:S(2)}) collective-permute-start(bf16[1,128,2,256]{1,3,2,0:T(8,128)(2,1)S(1)} %get-tuple-element.45), channel_id=1, source_target_pairs={{2,0},{4,2},{6,4},{8,6},{10,8},{12,10},{14,12},{16,14},{18,16},{20... | collective-permute-start | bytes 393224 | tf_op jit(solution)/shard_map/ppermute | solution.py:22
  61.1 1.3 copy-start.3
  61.2 1.6 copy-start.1
  61.2 1.8 copy-start.2
  62.1 164.2 %all-reduce.9.cloned.1.call-start = ((), (), s32[]{:S(2)}) async-start(), calls=%async_computation | async-start | bytes 2490368 | tf_op jit(solution)/shard_map/psum | solution.py:138
  136.8 8.6 %copy-start.8 = (bf16[2,128,128]{2,1,0:T(8,128)(2,1)S(1)}, bf16[2,128,128]{2,1,0:T(8,128)(2,1)}, u32[]{:S(2)}) copy-start(bf16[2,128,128]{2,1,0:T(8,128)(2,1)} %all_gather.7) | copy-start | bytes 196612
  226.3 2.0 copy-start.6
  226.3 2.9 %copy-start.12 = (f32[128,128]{1,0:T(8,128)S(1)}, f32[128,128]{1,0:T(8,128)}, u32[]{:S(2)}) copy-start(f32[128,128]{1,0:T(8,128)} %get-tuple-element.26) | copy-start | bytes 196612
  (5 other events, 3.8 us)
Sparse Core Ops, SparseCore 0:
  62.2 42.9 all-reduce.10
  135.7 90.4 all-reduce.8
